TPU v7x, 32 devices: a whole 2x2x4 slice. The times are simulated.
32 devices in a mesh: row: 4 (over y, core), col: 8 (over z, x).
Axes of the slice: x: 2, y: 2, z: 4, core: 2. Of those that a mesh axis runs over, the one named last changes fastest.
Arguments:
- support_views: float32 [256, 4, 3, 1024], P(('row', 'col')), may hold values from -6 to 6
- support_pick: int32 [256], P(('row', 'col')), may hold values from 0 to 3
- target_views: float32 [256, 4, 3, 1024], P(('row', 'col')), may hold values from -6 to 6
- target_pick: int32 [256], P(('row', 'col')), may hold values from 0 to 3
- support_labels: float32 [256, 10], P(('row', 'col')), may hold values from -6 to 6
- target_labels: int32 [256], replicated, may hold values from 0 to 9
Outputs:
- support_grad: float32 [256, 3, 1024], P(('row', 'col'))
- label_grad: float32 [256, 10], P(('row', 'col'))
- loss: float32 [], replicated
All inputs are finite; a program needn't handle non-finite values.
Results may differ from a plain program's by a relative error of at most 0.00055.
Values sent between devices are 32-bit elements; how exact they have to be, the bound alone decides.
No kernel may reach another device: no remote copies, remote signals or barrier semaphores. Data moves between devices by JAX's collectives and lax.ppermute only.
A program may use at most 64 MiB of HBM per device.

v0:
```python
import math
import jax
import jax.numpy as jnp
from jax import lax
from jax.sharding import PartitionSpec as P

SIDE = 32
LAYERS = 3
SUPPORT = 256
bias_variance = 0.1
ridge_scale = 0.1
highest = lax.Precision.HIGHEST


def shifted(surface, offset):
    extent = surface.shape[-1]
    padding = jnp.zeros(surface.shape[:-1] + (abs(offset),), surface.dtype)
    if offset > 0:
        return jnp.concatenate([surface[..., offset:], padding], axis=-1)
    return jnp.concatenate([padding, surface[..., : extent + offset]], axis=-1)


def average(surface):
    column = jnp.arange(surface.shape[-1], dtype=jnp.int32) % SIDE
    rightward = jnp.where(column < SIDE - 1, shifted(surface, 1), 0.0)
    leftward = jnp.where(column > 0, shifted(surface, -1), 0.0)
    across = surface + leftward + rightward
    return (across + shifted(across, SIDE) + shifted(across, -SIDE)) / 9.0


def choose_view(views, picked):
    options = jnp.arange(views.shape[1], dtype=jnp.int32)
    selector = (picked[:, None] == options[None, :]).astype(jnp.float32)
    return jnp.sum(selector[:, :, None, None] * views, axis=1)


def self_maps(images):
    energy = jnp.sum(images * images, axis=1) / images.shape[1]
    current = average(energy) + bias_variance
    stacked = [current]
    for layer in range(1, LAYERS):
        current = average(current) + bias_variance
        stacked.append(current)
    return jnp.stack(stacked, axis=1)


def self_back(images, grad_maps):
    carry = grad_maps[:, -1]
    for layer in range(grad_maps.shape[1] - 2, -1, -1):
        carry = grad_maps[:, layer] + average(carry)
    return average(carry)[:, None, :] * images * (2.0 / images.shape[1])


def arc(kernel_map, first_diag, second_diag):
    scale_map = jnp.sqrt(first_diag * second_diag)
    cosine = jnp.clip(kernel_map / scale_map, -1.0, 1.0)
    sine = jnp.sqrt(1.0 - cosine * cosine)
    angle = jnp.arccos(cosine)
    value = scale_map * (sine + (jnp.pi - angle) * cosine) / jnp.pi
    slope = (jnp.pi - angle) / jnp.pi
    spread = scale_map * sine / (2.0 * jnp.pi)
    return (value, slope, spread)


def pair_forward(first, first_maps, second, second_maps):
    product = first[:, None, 0] * second[None, :, 0]
    for channel in range(1, first.shape[1]):
        product = product + first[:, None, channel] * second[None, :, channel]
    current = average(product / first.shape[1]) + bias_variance
    slopes = []
    spreads = []
    depth = first_maps.shape[1]
    for layer in range(depth):
        value, slope, spread = arc(current, first_maps[:, None, layer], second_maps[None, :, layer])
        slopes.append(slope)
        spreads.append(spread)
        if layer + 1 < depth:
            current = average(value) + bias_variance
    return (jnp.mean(value, axis=-1), slopes, spreads)


def pair_backward(first, first_maps, second, second_maps, weights, want_second):
    kernel, slopes, spreads = pair_forward(first, first_maps, second, second_maps)
    depth = first_maps.shape[1]
    grad = jnp.broadcast_to(weights[:, :, None] / first.shape[-1], slopes[0].shape)
    first_parts = []
    second_parts = []
    for layer in range(depth - 1, -1, -1):
        scaled = grad * spreads[layer]
        first_parts.insert(0, jnp.sum(scaled, axis=1) / first_maps[:, layer])
        if want_second:
            second_parts.insert(0, jnp.sum(scaled, axis=0) / second_maps[:, layer])
        grad = average(grad * slopes[layer])
    first_image = (
        jnp.stack(
            [jnp.sum(grad * second[None, :, channel], axis=1) for channel in range(first.shape[1])],
            axis=1,
        )
        / first.shape[1]
    )
    if not want_second:
        return (first_image, jnp.stack(first_parts, axis=1), None, None)
    second_image = (
        jnp.stack(
            [jnp.sum(grad * first[:, None, channel], axis=0) for channel in range(first.shape[1])],
            axis=1,
        )
        / first.shape[1]
    )
    return (
        first_image,
        jnp.stack(first_parts, axis=1),
        second_image,
        jnp.stack(second_parts, axis=1),
    )


def blocked_kernel(first, first_maps, second, second_maps):
    block_width = math.gcd(second.shape[0], 4)
    block_count = second.shape[0] // block_width

    def one_block(inputs):
        part_images, part_maps = inputs
        kernel, _, _ = pair_forward(first, first_maps, part_images, part_maps)
        return kernel

    pieces = lax.map(
        one_block,
        (
            second.reshape((block_count, block_width) + second.shape[1:]),
            second_maps.reshape((block_count, block_width) + second_maps.shape[1:]),
        ),
    )
    return jnp.transpose(pieces, (1, 0, 2)).reshape(first.shape[0], second.shape[0])


def blocked_backward(first, first_maps, second, second_maps, weights, want_second):
    block_width = math.gcd(second.shape[0], 4)
    block_count = second.shape[0] // block_width
    block_weights = jnp.transpose(
        weights.reshape(first.shape[0], block_count, block_width), (1, 0, 2)
    )

    def one_block(carry, inputs):
        part_images, part_maps, part_weights = inputs
        grad_first, maps_first, grad_second, maps_second = pair_backward(
            first, first_maps, part_images, part_maps, part_weights, want_second
        )
        return ((carry[0] + grad_first, carry[1] + maps_first), (grad_second, maps_second))

    start = (jnp.zeros(first.shape, jnp.float32), jnp.zeros(first_maps.shape, jnp.float32))
    (first_grad, first_map_grad), (second_grad, second_map_grad) = lax.scan(
        one_block,
        start,
        (
            second.reshape((block_count, block_width) + second.shape[1:]),
            second_maps.reshape((block_count, block_width) + second_maps.shape[1:]),
            block_weights,
        ),
    )
    if not want_second:
        return (first_grad, first_map_grad, None, None)
    return (
        first_grad,
        first_map_grad,
        second_grad.reshape(second.shape),
        second_map_grad.reshape(second_maps.shape),
    )


def solve_with(factor, rhs):
    halfway = lax.linalg.triangular_solve(factor, rhs, left_side=True, lower=True)
    return lax.linalg.triangular_solve(
        factor, halfway, left_side=True, lower=True, transpose_a=True
    )


def assemble_folded(tiles, row_count, col_count, own_count, picks):
    span = col_count * own_count
    shaped = tiles.reshape(row_count, col_count, span, picks, own_count)
    block_ids = jnp.arange(row_count, dtype=jnp.int32)
    offsets = jnp.arange(picks, dtype=jnp.int32)
    selector = (
        block_ids[None, None, :] == (block_ids[:, None, None] + offsets[None, :, None]) % row_count
    ).astype(jnp.float32)
    upper = jnp.einsum("rcadk,rdq->raqck", shaped, selector, precision=highest)
    upper = upper.reshape(row_count * span, row_count * span)
    return upper + upper.T - jnp.diag(jnp.diag(upper))


def column_of(matrix, col_index, row_count, col_count, per_device):
    shaped = matrix.reshape(row_count, col_count, per_device, matrix.shape[-1])
    picked = lax.dynamic_index_in_dim(shaped, col_index, 1, keepdims=False)
    return picked.reshape(row_count * per_device, matrix.shape[-1])


def pick_blocks(stacked, row_index, row_count, own_count, picks):
    shaped = stacked.reshape((row_count, own_count) + stacked.shape[1:])
    rolled = jnp.roll(shaped, -row_index, axis=0)[:picks]
    return rolled.reshape((picks * own_count,) + stacked.shape[1:])


def place_blocks(picked, row_index, row_count, own_count, picks):
    shaped = picked.reshape((picks, own_count) + picked.shape[1:])
    padding = jnp.zeros((row_count - picks, own_count) + picked.shape[1:], picked.dtype)
    full = jnp.roll(jnp.concatenate([shaped, padding], axis=0), row_index, axis=0)
    return full.reshape((row_count * own_count,) + picked.shape[1:])


def body(support_views, support_pick, target_views, target_pick, support_labels, target_labels):
    row_count = lax.axis_size("row")
    col_count = lax.axis_size("col")
    row_index = lax.axis_index("row")
    col_index = lax.axis_index("col")
    own_count = support_views.shape[0]
    own_targets = target_views.shape[0]
    channels = support_views.shape[2]
    classes = support_labels.shape[1]
    own_support = choose_view(support_views, support_pick)
    own_target = choose_view(target_views, target_pick)
    support_pack = jnp.concatenate([own_support, self_maps(own_support)], axis=1)
    target_pack = jnp.concatenate([own_target, self_maps(own_target)], axis=1)
    row_pack = lax.all_gather(support_pack, "col", axis=0, tiled=True)
    column_pack, target_block = (
        lax.all_gather(support_pack, "row", axis=0, tiled=True),
        lax.all_gather(target_pack, "row", axis=0, tiled=True),
    )
    row_images = row_pack[:, :channels]
    row_maps = row_pack[:, channels:]
    column_images = column_pack[:, :channels]
    column_maps = column_pack[:, channels:]
    target_images = target_block[:, :channels]
    target_maps = target_block[:, channels:]
    row_start = row_index * col_count * own_count
    row_span = col_count * own_count
    half_count = row_count // 2
    picks = half_count + 1
    chosen_images = pick_blocks(column_images, row_index, row_count, own_count, picks)
    chosen_maps = pick_blocks(column_maps, row_index, row_count, own_count, picks)
    slot_ids = jnp.arange(picks * own_count, dtype=jnp.int32)
    offset_ids = slot_ids // own_count
    inner_ids = slot_ids % own_count
    local_cols = col_index * own_count + inner_ids
    chosen_global = (
        (row_index + offset_ids) % row_count * col_count + col_index
    ) * own_count + inner_ids
    row_ids = jnp.arange(row_span, dtype=jnp.int32)
    keep = jnp.where(
        offset_ids[None, :] == 0,
        row_ids[:, None] <= local_cols[None, :],
        jnp.where(offset_ids[None, :] == half_count, row_index < half_count, True),
    )
    keep_mask = keep.astype(jnp.float32)
    equal_mask = ((offset_ids[None, :] == 0) & (row_ids[:, None] == local_cols[None, :])).astype(
        jnp.float32
    )
    support_tile = blocked_kernel(row_images, row_maps, chosen_images, chosen_maps) * keep_mask
    cross_tile = blocked_kernel(row_images, row_maps, target_images, target_maps)
    onehot_all = (target_labels[:, None] == jnp.arange(classes, dtype=jnp.int32)[None, :]).astype(
        jnp.float32
    ) - 1.0 / classes
    identity = jnp.eye(SUPPORT, dtype=jnp.float32)
    tiles, all_labels = (
        lax.all_gather(support_tile, ("row", "col"), axis=0, tiled=True),
        lax.all_gather(support_labels, ("row", "col"), axis=0, tiled=True),
    )
    support_kernel = assemble_folded(tiles, row_count, col_count, own_count, picks)
    trace_mean = jnp.trace(support_kernel) / SUPPORT
    factor = jnp.linalg.cholesky(support_kernel + ridge_scale * trace_mean * identity)
    alpha = solve_with(factor, all_labels)
    alpha_rows = lax.dynamic_slice_in_dim(alpha, row_start, row_span, 0)
    labels_here = column_of(onehot_all, col_index, row_count, col_count, own_targets)
    predicted = lax.psum(jnp.dot(cross_tile.T, alpha_rows, precision=highest), "row")
    error = predicted - labels_here
    adjoint_part, loss_sum = lax.psum(
        (jnp.dot(cross_tile, error, precision=highest), jnp.sum(error * error)), "col"
    )
    adjoint = lax.all_gather(adjoint_part, "row", axis=0, tiled=True)
    gamma = solve_with(factor, adjoint)
    intersection = jnp.sum(gamma * alpha)
    gamma_rows = lax.dynamic_slice_in_dim(gamma, row_start, row_span, 0)
    cross_weights = jnp.dot(alpha_rows, error.T, precision=highest)
    alpha_chosen = alpha[chosen_global]
    gamma_chosen = gamma[chosen_global]
    folded = -(
        jnp.dot(gamma_rows, alpha_chosen.T, precision=highest)
        + jnp.dot(alpha_rows, gamma_chosen.T, precision=highest)
    )
    support_weights = (
        folded - equal_mask * (0.5 * folded + ridge_scale * intersection / SUPPORT)
    ) * keep_mask
    row_grad, row_map_grad, chosen_grad, chosen_map_grad = blocked_backward(
        row_images, row_maps, chosen_images, chosen_maps, support_weights, True
    )
    col_grad = place_blocks(chosen_grad, row_index, row_count, own_count, picks)
    col_map_grad = place_blocks(chosen_map_grad, row_index, row_count, own_count, picks)
    cross_grad, cross_map_grad, _, _ = blocked_backward(
        row_images, row_maps, target_images, target_maps, cross_weights, False
    )
    row_grad = row_grad + cross_grad
    row_map_grad = row_map_grad + cross_map_grad
    row_send = jnp.concatenate([row_grad, row_map_grad], axis=1)
    col_send = jnp.concatenate([col_grad, col_map_grad], axis=1)
    row_whole = lax.psum(row_send, "col")
    col_whole = lax.psum(col_send, "row")
    row_back = lax.dynamic_slice_in_dim(row_whole, col_index * own_count, own_count, 0)
    col_back = lax.dynamic_slice_in_dim(col_whole, row_index * own_count, own_count, 0)
    combined = row_back + col_back
    support_grad = combined[:, :channels] + self_back(own_support, combined[:, channels:])
    own_start = (row_index * col_count + col_index) * own_count
    label_grad = lax.dynamic_slice_in_dim(gamma, own_start, own_count, 0)
    return (support_grad, label_grad, 0.5 * loss_sum)


def solution(mesh):
    return jax.shard_map(
        body,
        mesh=mesh,
        in_specs=(
            P(("row", "col"), None, None, None),
            P(("row", "col")),
            P(("row", "col"), None, None, None),
            P(("row", "col")),
            P(("row", "col"), None),
            P(),
        ),
        out_specs=(P(("row", "col"), None, None), P(("row", "col"), None), P()),
        check_vma=False,
    )
```

profile of v0, /device:TPU:0, one launch (start us, length us, event | category | flops | bytes accessed | tf_op | source)
XLA Modules:
  0.0 1061.8 jit_solution(16985162748943276678)
XLA Ops:
  13.4 10.3 all_gather.19
  24.6 69.7 %all_gather.22 = f32[256,10]{1,0:T(8,128)S(1)} all-gather(f32[8,10]{1,0:T(8,128)S(1)} %copy-done.22), channel_id=1, replica_groups=mesh['row'=4,'col'=8] {'row','col'}, dimensions={0}, use_global_device_ids=true | all-gather | bytes 10560 | tf_op jit(solution)/shard_map/all_gather | solution.py:265
  94.9 7.8 all_gather.21
  107.6 80.1 %while.70 = (s32[]{:T(128)}, f32[6,64,4]{1,2,0:T(4,128)S(1)}, f32[64,3,1024]{2,0,1:T(8,128)S(1)}, f32[6,4,3,1024]{3,1,2,0:T(4,128)S(1)}, f32[64,3,1024]{2,0,1:T(...) while((s32[]{:T(128)}, f32[6,64,4]{1,2,0:T(4,128)S(1)}, f32[64,3,1024]{2,0,1:T(8,128)S(1)}, ...), condition=%wide.region_4.6_spmd, body=%wide.region_2.5_spmd.sunk | while | flops 19931136 | bytes 54733908 | solution.py:127
  117.9 3.1 multiply_reduce_fusion.27
  131.2 3.1 multiply_reduce_fusion.27
  140.2 3.0 multiply_multiply_fusion.26
  144.4 3.1 multiply_reduce_fusion.27
  157.7 3.1 multiply_reduce_fusion.27
  170.9 3.1 multiply_reduce_fusion.27
  184.2 3.1 multiply_reduce_fusion.27
  187.8 65.5 %all-gather = f32[32,64,24]{1,2,0:T(8,128)S(1)} all-gather(f32[1,64,24]{1,2,0:T(8,128)S(1)} %select_bitcast_fusion.1), channel_id=1, replica_groups=mesh['row'=4,'col'=8] {'row','col'}, dimensions={0}, use_global_device_ids=true | all-gather | bytes 202752 | tf_op jit(solution)/shard_map/all_gather | solution.py:264
  258.8 11.7 %cholesky.49 = f32[128,128]{1,0:T(8,128)S(1)} custom-call(f32[128,128]{1,0:T(8,128)S(1)} %cholesky.115), custom_call_target="Cholesky" | custom-call | tf_op jit(solution)/shard_map/jit(cholesky)/cholesky | solution.py:269
  270.6 9.8 custom-call.17
  280.9 11.7 %cholesky.103 = f32[128,128]{1,0:T(8,128)S(1)} custom-call(f32[128,128]{1,0:T(8,128)S(1)} %convolution_subtract_fusion), custom_call_target="Cholesky" | custom-call | tf_op jit(solution)/shard_map/jit(cholesky)/cholesky | solution.py:269
  295.7 4.3 while.74
  300.6 20.5 %custom-call.29 = f32[2,128,128]{1,2,0:T(8,128)S(1)} custom-call(f32[2,128,128]{2,1,0:T(8,128)} %copy-done.27), custom_call_target="InvertDiagBlocksLowerTriangular" | custom-call | tf_op jit(solution)/shard_map/triangular_solve/custom-call.4 | solution.py:173
  323.0 117.2 %while.71 = (s32[]{:T(128)}, f32[8,64,4]{1,2,0:T(4,128)}, f32[64,3,1024]{2,0,1:T(8,128)S(1)}, f32[8,4,3,1024]{3,1,2,0:T(4,128)}, f32[64,3,1024]{2,0,1:T(8,128)S(1)}, /*index=5*/f32[8,4,3,1024]{3,1,2,0:T(4,128)}, s32[]{:T(128)}) while((s32[]{:T(128)}, f32[8,64,4]{1,2,0:T(4,128)}, f32[64,3,1024]{2,0,1:T(8,128)S(1)}, ...), condition=%wide.region_14.16_spmd, body=%wide.region_12.15_spmd.sunk | while | flops 19931136 | bytes 54733392 | solution.py:127
  334.1 3.1 multiply_reduce_fusion.28
  348.7 3.1 multiply_reduce_fusion.28
  363.4 3.1 multiply_reduce_fusion.28
  378.0 3.1 multiply_reduce_fusion.28
  392.6 3.1 multiply_reduce_fusion.28
  407.2 3.1 multiply_reduce_fusion.28
  421.8 3.1 multiply_reduce_fusion.28
  436.5 3.1 multiply_reduce_fusion.28
  443.1 6.6 psum.35
  454.0 20.6 %all-reduce.111 = (f32[64,10]{0,1:T(8,128)S(1)}, f32[]{:T(128)}) all-reduce(f32[64,10]{0,1:T(8,128)} %fusion.91, f32[]{:T(128)} %multiply_reduce_fusion.19), channel_id=1, replica_groups=mesh['row'=4,'col'=8] {'col'}, use_global_device_ids=true, to_apply=%region_16.20 | all-reduce | flops 641 | bytes 5128 | tf_op jit(solution)/shard_map/psum | solution.py:275
  474.6 5.2 all-gather.1
  489.0 222.6 %while.72 = (s32[]{:T(128)}, f32[64,3,1024]{2,0,1:T(8,128)S(1)}, f32[64,3,1024]{2,0,1:T(8,128)S(1)}, f32[6,4,3,1024]{3,1,0,2:T(4,128)}, f32[6,4,3,1024]{3,1,0,2:...) while((s32[]{:T(128)}, f32[64,3,1024]{2,0,1:T(8,128)S(1)}, ...), condition=%wide.region_31.35_spmd.clone, body=%wide.region_18.34_spmd.clone.sunk | while | flops 38808064 | bytes 129204872 | solution.py:152
  719.3 243.5 %while.73 = (s32[]{:T(128)}, f32[64,3,1024]{2,0,1:T(8,128)S(1)}, f32[64,3,1024]{2,0,1:T(8,128)S(1)}, f32[64,3,1024]{2,0,1:T(8,128)S(1)}, f32[8,4,3,1024]{3,1,2,0...) while((s32[]{:T(128)}, f32[64,3,1024]{2,0,1:T(8,128)S(1)}, ...), condition=%wide.region_39.43_spmd.clone, body=%wide.region_32.42_spmd.clone.sunk | while | flops 36203008 | bytes 120111224 | solution.py:152
  967.8 83.4 %all-reduce.115.cloned.1.call-done = f32[64,6,1024]{2,0,1:T(8,128)} async-done(((f32[64,6,1024]{2,0,1:T(8,128)}), f32[64,6,1024]{2,0,1:T(8,128)}) %all-reduce.115.cloned.1.call-update) | async-done | bytes 1572880 | tf_op jit(solution)/shard_map/psum | solution.py:304
  (1042 shorter events, 632.2 us)
Async XLA Ops:
  7.2 3.4 copy-start.11
  7.2 99.0 %all-gather.4.cloned.1.call-start = ((), (), s32[]{:S(2)}) async-start(), calls=%async_computation | async-start | bytes 1769472 | tf_op jit(solution)/shard_map/all_gather | solution.py:223
  7.2 4.8 copy-start.17
  7.2 4.8 copy-start.19
  10.9 1.6 copy-start.9
  13.4 954.4 %all-reduce.117.cloned.1.call-start = ((), (), s32[]{:S(2)}) async-start(), calls=%async_computation.2 | async-start | bytes 1572864 | tf_op jit(solution)/shard_map/psum | solution.py:305
  23.9 0.7 copy-start.22
  102.8 1.8 copy-start.23
  105.5 82.2 %copy-start.24 = (s32[24]{0:T(128)}, s32[24]{0:T(128)S(1)}, u32[]{:S(2)}) copy-start(s32[24]{0:T(128)S(1)} %fusion.81) | copy-start | bytes 292
  105.5 82.2 %copy-start.25 = (pred[24]{0:T(512)(128)(4,1)}, pred[24]{0:T(512)(128)(4,1)S(1)}, u32[]{:S(2)}) copy-start(pred[24]{0:T(512)(128)(4,1)S(1)} %get-tuple-element.1339) | copy-start | bytes 76
  105.5 82.2 %copy-start.26 = (pred[24]{0:T(512)(128)(4,1)}, pred[24]{0:T(512)(128)(4,1)S(1)}, u32[]{:S(2)}) copy-start(pred[24]{0:T(512)(128)(4,1)S(1)} %get-tuple-element.1340) | copy-start | bytes 76
  187.7 66.6 %copy-start.7 = (f32[6,4,3,1024]{3,1,2,0:T(4,128)}, f32[6,4,3,1024]{3,1,2,0:T(4,128)S(1)}, u32[]{:S(2)}) copy-start(f32[6,4,3,1024]{3,1,2,0:T(4,128)S(1)} %get-tuple-element.2067) | copy-start | bytes 884740
  187.7 66.9 %copy-start.8 = (f32[6,4,3,1024]{3,1,2,0:T(4,128)}, f32[6,4,3,1024]{3,1,2,0:T(4,128)S(1)}, u32[]{:S(2)}) copy-start(f32[6,4,3,1024]{3,1,2,0:T(4,128)S(1)} %get-tuple-element.2068) | copy-start | bytes 884740
  300.0 0.6 copy-start.27
  323.0 126.7 %copy-start.16 = (f32[32,10]{0,1:T(8,128)S(1)}, f32[32,10]{0,1:T(8,128)}, u32[]{:S(2)}) copy-start(f32[32,10]{0,1:T(8,128)} %reshape.516) | copy-start | bytes 3844
  440.2 48.8 %copy-start.2 = (f32[64,3,1024]{2,0,1:T(8,128)S(1)}, f32[64,3,1024]{2,0,1:T(8,128)}, u32[]{:S(2)}) copy-start(f32[64,3,1024]{2,0,1:T(8,128)} %custom-call.22) | copy-start | bytes 2359300
  440.2 48.8 %copy-start.4 = (f32[64,3,1024]{2,0,1:T(8,128)S(1)}, f32[64,3,1024]{2,0,1:T(8,128)}, u32[]{:S(2)}) copy-start(f32[64,3,1024]{2,0,1:T(8,128)} %custom-call.23) | copy-start | bytes 2359300
  441.1 0.6 copy-start.21
  483.9 5.1 copy-start.12
  484.3 4.7 copy-start.14
  711.7 5.8 copy-start.3
  711.7 5.8 copy-start.5
  717.6 1.2 copy-start
  717.6 1.6 copy-start.1
  718.7 332.5 %all-reduce.115.cloned.1.call-start = ((), (), s32[]{:S(2)}) async-start(), calls=%async_computation.1 | async-start | bytes 3145728 | tf_op jit(solution)/shard_map/psum | solution.py:304
  962.8 1.4 copy-start.6
  965.6 0.7 copy-start.13
  965.6 0.7 copy-start.15
  965.6 86.7 %copy-start.18 = (pred[1024]{0:T(1024)(128)(4,1)S(1)}, pred[1024]{0:T(1024)(128)(4,1)}, u32[]{:S(2)}) copy-start(pred[1024]{0:T(1024)(128)(4,1)} %copy-done.17) | copy-start | bytes 3076
  965.6 86.7 %copy-start.20 = (pred[1024]{0:T(1024)(128)(4,1)S(1)}, pred[1024]{0:T(1024)(128)(4,1)}, u32[]{:S(2)}) copy-start(pred[1024]{0:T(1024)(128)(4,1)} %copy-done.19) | copy-start | bytes 3076
  965.6 87.6 %copy-start.10 = (f32[8,3,1024]{2,1,0:T(4,128)S(1)}, f32[8,3,1024]{2,1,0:T(4,128)}, u32[]{:S(2)}) copy-start(f32[8,3,1024]{2,1,0:T(4,128)} %copy-done.9) | copy-start | bytes 294916
Sparse Core Ops, SparseCore 0:
  13.5 47.3 all-gather.3
  718.8 31.1 all-reduce.116
  965.7 85.3 all-reduce.114
where the time goes:
time: 1070 us; the launch traced here: 1060 us
  other arithmetic  564 us (53%)
  blocking collectives  186 us (17%)
  local copies, waits for them, and re-layouts  158 us (15%)
  waiting for transfers between devices  83.5 us (8%)
  loops' own time  41.1 us (4%)
  between operations  19.1 us (2%)
  matrix products  11 us (1%)
    div x56, other arithmetic, arc(): value = scale_map * (sine + (jnp.pi - angle) * cosine) / jnp.pi  165 us
    psum x1, waiting for transfers between devices, body(): row_whole = lax.psum(row_send, 'col')  83.4 us
    add x133, other arithmetic, average(): across = surface + leftward + rightward  83.2 us
    all_gather x1, blocking collectives, body(): lax.all_gather(support_labels, ('row', 'col'), axis=0, tiled=True)  69.7 us
    all_gather x1, blocking collectives, body(): lax.all_gather(support_tile, ('row', 'col'), axis=0, tiled=True)  65.5 us
    mul x40, other arithmetic, pair_backward(): grad = average(grad * slopes[layer])  56.8 us
    reduce_sum x24, other arithmetic, pair_backward(): first_parts.insert(0, jnp.sum(scaled, axis=1) / first_maps[:, layer])  53.7 us
    slice x135, local copies, waits for them, and re-layouts, shifted(): return jnp.concatenate([padding, surface[..., :extent + offset]], axis=-1)  49 us
  transfers between devices with their start and end apart: 3, of which 1 were waited for; matrix products, arithmetic and copies ran while one was open for 24% of the time, Pallas kernels for 0%

commit v1 on v0

--- a/solution.py
+++ b/solution.py
@@ -301,7 +301,14 @@
     row_map_grad = row_map_grad + cross_map_grad
     row_send = jnp.concatenate([row_grad, row_map_grad], axis=1)
     col_send = jnp.concatenate([col_grad, col_map_grad], axis=1)
-    row_whole = lax.psum(row_send, "col")
+    row_whole, local_now = (row_send, 0)
+    workers = jax.lax.axis_size("col")
+    while 1 << local_now < workers:
+        carry_in = jax.lax.ppermute(
+            row_whole, "col", perm=tuple(((ii, ii ^ 1 << local_now) for ii in range(workers)))
+        )
+        row_whole = row_whole + carry_in
+        local_now = local_now + 1
     col_whole = lax.psum(col_send, "row")
     row_back = lax.dynamic_slice_in_dim(row_whole, col_index * own_count, own_count, 0)
     col_back = lax.dynamic_slice_in_dim(col_whole, row_index * own_count, own_count, 0)

time: 1070 us -> 1120 us (1.047)
  waiting for transfers between devices: 83.5 us -> 139 us
    ppermute x0 -> x3, waiting for transfers between devices: none -> 106 us  [body(): jax.lax.ppermute(row_whole, 'col', perm=tuple(((ii, ii ^ 1 << local_now)...]
    psum x1 -> x0, waiting for transfers between devices: 83.4 us -> none  [body(): row_whole = lax.psum(row_send, 'col')]
    psum x1, waiting for transfers between devices: 0.02 us -> 33.2 us  [body(): col_whole = lax.psum(col_send, 'row')]
    add x14, other arithmetic: 24.2 us -> 6.91 us  [one_block(): carry[0] + grad_first]
  transfers between devices with their start and end apart: 3 -> 5, of which waited for: 1 -> 4; matrix products, arithmetic and copies ran while one was open for 24% -> 1% of each run, Pallas kernels for 0% -> 0%
where the time goes in v1:
time: 1120 us; the launch traced here: 1110 us
  other arithmetic  568 us (51%)
  blocking collectives  185 us (17%)
  local copies, waits for them, and re-layouts  152 us (14%)
  waiting for transfers between devices  139 us (12%)
  loops' own time  41.7 us (4%)
  between operations  19.5 us (2%)
    div x56, other arithmetic, arc(): value = scale_map * (sine + (jnp.pi - angle) * cosine) / jnp.pi  165 us
    ppermute x3, waiting for transfers between devices, body(): jax.lax.ppermute(row_whole, 'col', perm=tuple(((ii, ii ^ 1 << local_now)...  106 us
    add x133, other arithmetic, average(): across = surface + leftward + rightward  83 us
    all_gather x1, blocking collectives, body(): lax.all_gather(support_labels, ('row', 'col'), axis=0, tiled=True)  69.6 us
    all_gather x1, blocking collectives, body(): lax.all_gather(support_tile, ('row', 'col'), axis=0, tiled=True)  65.5 us
    reduce_sum x24, other arithmetic, pair_backward(): first_parts.insert(0, jnp.sum(scaled, axis=1) / first_maps[:, layer])  64.3 us
    mul x40, other arithmetic, pair_backward(): grad = average(grad * slopes[layer])  60.9 us
    slice x135, local copies, waits for them, and re-layouts, shifted(): return jnp.concatenate([padding, surface[..., :extent + offset]], axis=-1)  49.3 us
  transfers between devices with their start and end apart: 5, of which 4 were waited for; matrix products, arithmetic and copies ran while one was open for 1% of the time, Pallas kernels for 0%

profile of v1, /device:TPU:0, one launch (start us, length us, event | category | flops | bytes accessed | tf_op | source)
XLA Modules:
  0.0 1110.5 jit_solution(9018393693677615733)
XLA Ops:
  13.4 10.3 all_gather.19
  25.0 69.6 %all_gather.22 = f32[256,10]{1,0:T(8,128)S(1)} all-gather(f32[8,10]{1,0:T(8,128)S(1)} %copy-done.32), channel_id=1, replica_groups=mesh['row'=4,'col'=8] {'row','col'}, dimensions={0}, use_global_device_ids=true | all-gather | bytes 10560 | tf_op jit(solution)/shard_map/all_gather | solution.py:265
  95.9 7.8 all_gather.21
  107.4 84.7 %while.70 = (s32[]{:T(128)}, f32[6,64,4]{1,2,0:T(4,128)S(1)}, f32[64,3,1024]{2,0,1:T(8,128)S(1)}, f32[6,4,3,1024]{3,1,2,0:T(4,128)S(1)}, f32[64,3,1024]{2,0,1:T(...) while((s32[]{:T(128)}, f32[6,64,4]{1,2,0:T(4,128)S(1)}, f32[64,3,1024]{2,0,1:T(8,128)S(1)}, ...), condition=%wide.region_4.6_spmd, body=%wide.region_2.5_spmd.sunk | while | flops 19931136 | bytes 54733916 | solution.py:127
  192.2 65.5 %all-gather = f32[32,64,24]{1,2,0:T(8,128)S(1)} all-gather(f32[1,64,24]{1,2,0:T(8,128)S(1)} %select_bitcast_fusion.1), channel_id=1, replica_groups=mesh['row'=4,'col'=8] {'row','col'}, dimensions={0}, use_global_device_ids=true | all-gather | bytes 202752 | tf_op jit(solution)/shard_map/all_gather | solution.py:264
  263.2 11.7 %cholesky.49 = f32[128,128]{1,0:T(8,128)S(1)} custom-call(f32[128,128]{1,0:T(8,128)S(1)} %cholesky.115), custom_call_target="Cholesky" | custom-call | tf_op jit(solution)/shard_map/jit(cholesky)/cholesky | solution.py:269
  275.0 9.8 custom-call.17
  285.4 11.7 %cholesky.103 = f32[128,128]{1,0:T(8,128)S(1)} custom-call(f32[128,128]{1,0:T(8,128)S(1)} %convolution_subtract_fusion), custom_call_target="Cholesky" | custom-call | tf_op jit(solution)/shard_map/jit(cholesky)/cholesky | solution.py:269
  300.1 5.5 while.74
  305.6 20.5 %custom-call.29 = f32[2,128,128]{1,2,0:T(8,128)S(1)} custom-call(f32[2,128,128]{2,1,0:T(8,128)} %get-tuple-element.627), custom_call_target="InvertDiagBlocksLowerTriangular" | custom-call | tf_op jit(solution)/shard_map/triangular_solve/custom-call.4 | solution.py:173
  327.3 106.1 %while.71 = (s32[]{:T(128)}, f32[8,64,4]{1,2,0:T(4,128)S(1)}, f32[64,3,1024]{2,0,1:T(8,128)S(1)}, f32[8,4,3,1024]{3,1,2,0:T(4,128)S(1)}, f32[64,3,1024]{2,0,1:T(...) while((s32[]{:T(128)}, f32[8,64,4]{1,2,0:T(4,128)S(1)}, f32[64,3,1024]{2,0,1:T(8,128)S(1)}, ...), condition=%wide.region_14.16_spmd, body=%wide.region_12.15_spmd.sunk | while | flops 19931136 | bytes 54733916 | solution.py:127
  433.6 5.8 psum.28
  441.0 20.4 %all-reduce.111 = (f32[64,10]{0,1:T(8,128)S(1)}, f32[]{:T(128)}) all-reduce(f32[64,10]{0,1:T(8,128)S(1)} %fusion.92, f32[]{:T(128)} %multiply_reduce_fusion.19), channel_id=1, replica_groups=mesh['row'=4,'col'=8] {'col'}, use_global_device_ids=true, to_apply=%region_16.20 | all-reduce | flops 641 | bytes 5128 | tf_op jit(solution)/shard_map/psum | solution.py:275
  461.4 5.2 all-gather.1
  471.9 236.0 %while.72 = (s32[]{:T(128)}, f32[64,3,1024]{2,0,1:T(8,128)}, f32[64,3,1024]{2,0,1:T(8,128)}, f32[6,4,3,1024]{3,1,0,2:T(4,128)}, f32[6,4,3,1024]{3,1,0,2:T(4,128)...) while((s32[]{:T(128)}, f32[64,3,1024]{2,0,1:T(8,128)}, ...), condition=%wide.region_31.35_spmd.clone, body=%wide.region_18.34_spmd.clone.sunk | while | flops 38808064 | bytes 144933232 | solution.py:152
  707.9 247.1 %while.73 = (s32[]{:T(128)}, f32[64,3,1024]{2,0,1:T(8,128)S(1)}, f32[64,3,1024]{2,0,1:T(8,128)S(1)}, f32[64,3,1024]{2,0,1:T(8,128)S(1)}, f32[8,4,3,1024]{3,1,2,0...) while((s32[]{:T(128)}, f32[64,3,1024]{2,0,1:T(8,128)S(1)}, ...), condition=%wide.region_39.43_spmd.clone, body=%wide.region_32.42_spmd.clone.sunk | while | flops 36203008 | bytes 123257048 | solution.py:152
  726.2 3.5 multiply_reduce_fusion.31
  731.0 3.5 multiply_reduce_fusion.32
  757.1 3.5 multiply_reduce_fusion.31
  761.9 3.5 multiply_reduce_fusion.32
  788.0 3.5 multiply_reduce_fusion.31
  792.7 3.5 multiply_reduce_fusion.32
  818.9 3.5 multiply_reduce_fusion.31
  823.6 3.5 multiply_reduce_fusion.32
  854.5 3.5 multiply_reduce_fusion.32
  885.4 3.5 multiply_reduce_fusion.32
  916.3 3.5 multiply_reduce_fusion.32
  947.2 3.5 multiply_reduce_fusion.32
  956.7 36.6 %collective-permute-done = f32[64,6,1024]{2,0,1:T(8,128)S(1)} collective-permute-done((f32[64,6,1024]{2,0,1:T(8,128)S(1)}, f32[64,6,1024]{2,0,1:T(8,128)S(1)}, u32[]{:S(2)}, u32[]{:S(2)}) %collective-permute-start) | collective-permute-done | bytes 1572896 | tf_op jit(solution)/shard_map/ppermute | solution.py:307
  993.8 35.8 %collective-permute-done.1 = f32[64,6,1024]{2,0,1:T(8,128)S(1)} collective-permute-done((f32[64,6,1024]{2,0,1:T(8,128)S(1)}, f32[64,6,1024]{2,0,1:T(8,128)S(1)}, u32[]{:S(2)}, u32[]{:S(2)}) %collective-permute-start.1) | collective-permute-done | bytes 1572896 | tf_op jit(solution)/shard_map/ppermute | solution.py:307
  1032.8 33.2 %all-reduce.114.cloned.1.call-done = f32[32,6,1024]{2,0,1:T(8,128)} async-done(((f32[32,6,1024]{2,0,1:T(8,128)}), f32[32,6,1024]{2,0,1:T(8,128)}) %all-reduce.114.cloned.1.call-update) | async-done | bytes 786448 | tf_op jit(solution)/shard_map/psum | solution.py:312
  1066.0 33.5 %collective-permute-done.2 = f32[64,6,1024]{2,0,1:T(8,128)} collective-permute-done((f32[64,6,1024]{2,0,1:T(8,128)S(1)}, f32[64,6,1024]{2,0,1:T(8,128)}, u32[]{:S(2)}, u32[]{:S(2)}) %collective-permute-start.2) | collective-permute-done | bytes 1572896 | tf_op jit(solution)/shard_map/ppermute | solution.py:307
  (1171 shorter events, 629.8 us)
Async XLA Ops:
  7.2 3.4 copy-start.20
  7.2 98.8 %all-gather.4.cloned.1.call-start = ((), (), s32[]{:S(2)}) async-start(), calls=%async_computation | async-start | bytes 1769472 | tf_op jit(solution)/shard_map/all_gather | solution.py:223
  7.2 4.8 copy-start.28
  7.2 4.8 copy-start.30
  13.4 1052.7 %all-reduce.114.cloned.1.call-start = ((), (), s32[]{:S(2)}) async-start(), calls=%async_computation.1 | async-start | bytes 1572864 | tf_op jit(solution)/shard_map/psum | solution.py:312
  192.1 66.5 %copy-start.13 = (f32[6,4,3,1024]{3,1,2,0:T(4,128)}, f32[6,4,3,1024]{3,1,2,0:T(4,128)S(1)}, u32[]{:S(2)}) copy-start(f32[6,4,3,1024]{3,1,2,0:T(4,128)S(1)} %get-tuple-element.2065) | copy-start | bytes 884740
  298.7 27.5 %copy-start.19 = (f32[256,10]{1,0:T(8,128)S(1)}, f32[256,10]{1,0:T(8,128)}, u32[]{:S(2)}) copy-start(f32[256,10]{1,0:T(8,128)} %copy-done.18) | copy-start | bytes 30724
  327.3 112.1 %copy-start.27 = (f32[32,10]{0,1:T(8,128)S(1)}, f32[32,10]{0,1:T(8,128)}, u32[]{:S(2)}) copy-start(f32[32,10]{0,1:T(8,128)} %reshape.516) | copy-start | bytes 3844
  433.4 38.4 %copy-start.16 = (f32[8,4,3,1024]{3,1,2,0:T(4,128)}, f32[8,4,3,1024]{3,1,2,0:T(4,128)S(1)}, u32[]{:S(2)}) copy-start(f32[8,4,3,1024]{3,1,2,0:T(4,128)S(1)} %get-tuple-element.2066) | copy-start | bytes 1179652
  433.4 38.4 %copy-start.17 = (f32[8,4,3,1024]{3,1,2,0:T(4,128)}, f32[8,4,3,1024]{3,1,2,0:T(4,128)S(1)}, u32[]{:S(2)}) copy-start(f32[8,4,3,1024]{3,1,2,0:T(4,128)S(1)} %get-tuple-element.2067) | copy-start | bytes 1179652
  467.4 4.5 copy-start.23
  467.8 4.0 copy-start.25
  471.9 236.0 %copy-start = (f32[64,3,1024]{2,0,1:T(8,128)S(1)}, f32[64,3,1024]{2,0,1:T(8,128)}, u32[]{:S(2)}) copy-start(f32[64,3,1024]{2,0,1:T(8,128)} %custom-call.24) | copy-start | bytes 2359300
  471.9 236.0 %copy-start.1 = (f32[64,3,1024]{2,0,1:T(8,128)S(1)}, f32[64,3,1024]{2,0,1:T(8,128)}, u32[]{:S(2)}) copy-start(f32[64,3,1024]{2,0,1:T(8,128)} %custom-call.25) | copy-start | bytes 2359300
  519.5 1.7 copy-start.8
  519.5 1.7 copy-start.9
  552.8 1.7 copy-start.8
  552.8 1.7 copy-start.9
  586.1 1.7 copy-start.8
  586.1 1.7 copy-start.9
  619.4 1.7 copy-start.8
  619.4 1.7 copy-start.9
  652.7 1.7 copy-start.9
  686.0 1.7 copy-start.9
  956.6 36.7 %collective-permute-start = (f32[64,6,1024]{2,0,1:T(8,128)S(1)}, f32[64,6,1024]{2,0,1:T(8,128)S(1)}, u32[]{:S(2)}, u32[]{:S(2)}) collective-permute-start(f32[64,6,1024]{2,0,1:T(8,128)S(1)} %pad_maximum_fusion), channel_id=1, source_target_pairs={{0,1},{1,0},{2,3},{3,2},{4,5},{5,4},{6,7},{7,6},{8,9},{9,8},{10,11... | collective-permute-start | bytes 4718600 | tf_op jit(solution)/shard_map/ppermute | solution.py:307
  993.7 36.2 %copy-start.22 = (f32[6,4,3,1024]{3,1,0,2:T(4,128)S(1)}, f32[6,4,3,1024]{3,1,0,2:T(4,128)}, u32[]{:S(2)}) copy-start(f32[6,4,3,1024]{3,1,0,2:T(4,128)} %get-tuple-element.535) | copy-start | bytes 884740
  993.7 36.4 %copy-start.21 = (f32[6,4,3,1024]{3,1,0,2:T(4,128)S(1)}, f32[6,4,3,1024]{3,1,0,2:T(4,128)}, u32[]{:S(2)}) copy-start(f32[6,4,3,1024]{3,1,0,2:T(4,128)} %get-tuple-element.534) | copy-start | bytes 884740
  993.7 35.8 %collective-permute-start.1 = (f32[64,6,1024]{2,0,1:T(8,128)S(1)}, f32[64,6,1024]{2,0,1:T(8,128)S(1)}, u32[]{:S(2)}, u32[]{:S(2)}) collective-permute-start(f32[64,6,1024]{2,0,1:T(8,128)S(1)} %fusion.94), channel_id=1, source_target_pairs={{0,2},{1,3},{2,0},{3,1},{4,6},{5,7},{6,4},{7,5},{8,10},{9,11},{10,... | collective-permute-start | bytes 4718600 | tf_op jit(solution)/shard_map/ppermute | solution.py:307
  1029.8 69.7 %collective-permute-start.2 = (f32[64,6,1024]{2,0,1:T(8,128)S(1)}, f32[64,6,1024]{2,0,1:T(8,128)}, u32[]{:S(2)}, u32[]{:S(2)}) collective-permute-start(f32[64,6,1024]{2,0,1:T(8,128)S(1)} %add.1688), channel_id=1, source_target_pairs={{0,4},{1,5},{2,6},{3,7},{4,0},{5,1},{6,2},{7,3},{8,12},{9,13},{10,... | collective-permute-start | bytes 4718600 | tf_op jit(solution)/shard_map/ppermute | solution.py:307
  1030.5 70.2 %copy-start.29 = (pred[1024]{0:T(1024)(128)(4,1)S(1)}, pred[1024]{0:T(1024)(128)(4,1)}, u32[]{:S(2)}) copy-start(pred[1024]{0:T(1024)(128)(4,1)} %copy-done.28) | copy-start | bytes 3076
  1030.5 70.2 %copy-start.31 = (pred[1024]{0:T(1024)(128)(4,1)S(1)}, pred[1024]{0:T(1024)(128)(4,1)}, u32[]{:S(2)}) copy-start(pred[1024]{0:T(1024)(128)(4,1)} %copy-done.30) | copy-start | bytes 3076
  1031.5 70.1 %copy-start.15 = (f32[8,3,1024]{2,1,0:T(4,128)S(1)}, f32[8,3,1024]{2,1,0:T(4,128)}, u32[]{:S(2)}) copy-start(f32[8,3,1024]{2,1,0:T(4,128)} %copy-done.14) | copy-start | bytes 294916
  (63 other events, 80.1 us)
Sparse Core Ops, SparseCore 0:
  13.5 47.3 all-gather.3
  1031.6 34.3 all-reduce.113
